TPU v7x, 512 devices: a whole 4x4x16 slice. The times are simulated.
512 devices in a mesh: head: 16 (over z), ctx: 32 (over x, y, core).
Axes of the slice: x: 4, y: 4, z: 16, core: 2. Of those that a mesh axis runs over, the one named last changes fastest.
Arguments:
- x_mant: bfloat16 [4096, 16384], P('ctx', 'head'), may hold values from -4 to 4
- x_codes: int32 [4096, 512], P('ctx', 'head'), may hold values from -2 to 2
- bc_raw: bfloat16 [4096, 2048], P('ctx'), may hold values from -5 to 5
- gate_z: bfloat16 [4096, 16384], P('ctx', 'head'), may hold values from -5 to 5
- conv_x: float32 [4, 16384], P(None, 'head'), may hold values from -3 to 3
- conv_bc: float32 [4, 2048], replicated, may hold values from -3 to 3
- dt_raw: float32 [4096, 256], P('ctx', 'head'), may hold values from -4 to 4
- a_log: float32 [256], P('head'), as said below
- d_skip: float32 [256], P('head'), may hold values from 0.5 to 1.5
- norm_gain: float32 [16384], P('head'), may hold values from 0.5 to 1.5
- prompt_lengths: int32 [4], replicated, may hold values from 1 to 2112, 4096 in all
- cache_slot: int32 [4], replicated, may hold values from 0 to 63, as said below
- prefix_state: bfloat16 [64, 16384, 128], P('ctx', 'head'), may hold values from -5 to 5
- tail_x: bfloat16 [64, 3, 16384], P('ctx', None, 'head'), may hold values from -5 to 5
- tail_bc: bfloat16 [64, 3, 2048], P('ctx'), may hold values from -5 to 5
Outputs:
- mixed: bfloat16 [4096, 16384], P('ctx', 'head')
Inputs may be any that keep to these rules, and one draw needn't show every extreme that they name: `prompt_lengths`: the lengths sum to 4096, and the longest is exactly 2112. `cache_slot`: slot 63 is read by some prompt and slot 0 by another; prompts may share a slot. `a_log`: log of a positive rate per head.
All inputs are finite; a program needn't handle non-finite values.
Results may differ from a plain program's by a relative error of at most 0.0065.
Values may be sent and summed in bfloat16 or wider, within the bound.
No kernel may reach another device: no remote copies, remote signals or barrier semaphores. Data moves between devices by JAX's collectives and lax.ppermute only.
A program may use at most 64 MiB of HBM per device.

v0:
```python
import jax
import jax.numpy as jnp
from jax import lax
from jax.sharding import PartitionSpec as P

HEADS = 256
GROUPS = 8
eps_norm = 1e-05


def passed_along(array, axis, by):
    devices = lax.axis_size(axis)
    pairs = [(i, i + by) for i in range(devices) if 0 <= i + by < devices]
    return lax.ppermute(array, axis, pairs)


def from_root(value, axis, source):
    kept = jnp.where(lax.axis_index(axis) == source, value, 0).astype(value.dtype)
    return lax.psum(kept, axis)


def entering(array, axis, combine, identity):
    devices, index = (lax.axis_size(axis), lax.axis_index(axis))
    everything = jax.tree.map(lambda part: lax.all_gather(part, axis), array)
    start = jax.tree.map(
        lambda part, zero: jnp.broadcast_to(jnp.asarray(zero, part.dtype), part.shape),
        array,
        identity,
    )

    def hop(k, before):
        reached = k < index
        new = combine(before, jax.tree.map(lambda part: part[k], everything))
        return jax.tree.map(lambda a, b: jnp.where(reached, a, b), new, before)

    return lax.fori_loop(0, devices, hop, start)


def dequant(mantissa, codes):
    row_count, chan_count = mantissa.shape
    block_count = codes.shape[1]
    scaled = mantissa.astype(jnp.float32).reshape(row_count, block_count, chan_count // block_count)
    scaled = scaled * jnp.exp2(codes.astype(jnp.float32))[:, :, None]
    return scaled.reshape(row_count, chan_count)


def prompt_rows(starts, offset, row_count):
    position = jnp.arange(row_count, dtype=jnp.int32) + offset
    inside = (position[:, None] >= starts[None, :]).astype(jnp.int32)
    return jnp.sum(inside, axis=1) - 1


def pick_rows(table, prompt_id):
    hit = prompt_id[:, None] == jnp.arange(table.shape[0], dtype=jnp.int32)[None, :]
    return jnp.sum(jnp.where(hit, table[None, :], 0), axis=1)


def causal_conv(current, previous, tails, weights, prompt_id, start_loc):
    row_count, chan_count = current.shape
    lag_count = previous.shape[0]
    prompt_count = tails.shape[0]
    extended = jnp.concatenate([previous, current], axis=0)
    flat_tails = tails.reshape(prompt_count * lag_count, chan_count)
    row_start = pick_rows(start_loc, prompt_id)
    position = jnp.arange(row_count, dtype=jnp.int32)
    total = jnp.zeros((row_count, chan_count), jnp.float32)
    for shift_by in range(lag_count + 1):
        source = extended[lag_count - shift_by : lag_count - shift_by + row_count]
        earlier = position - shift_by
        index = prompt_id * lag_count + jnp.clip(earlier - row_start + lag_count, 0, lag_count - 1)
        tail_rows = jnp.take(flat_tails, index, axis=0)
        value = jnp.where((earlier < row_start)[:, None], tail_rows, source)
        total = total + weights[lag_count - shift_by][None, :] * value
    return total


def span_local(x_act, b_act, c_act, delta, log_decay, prompt_id, start_loc, prefixes):
    row_count, head_count, width = x_act.shape
    group_count, state = (b_act.shape[1], b_act.shape[2])
    per_group = head_count // group_count
    cumul = jnp.cumsum(log_decay, axis=0)
    before_sum = cumul - log_decay
    position = jnp.arange(row_count, dtype=jnp.int32)
    live = (prompt_id[:, None] == prompt_id[None, :]) & (position[:, None] >= position[None, :])
    scores = jnp.einsum("tgn,sgn->gts", c_act, b_act, preferred_element_type=jnp.float32)

    def one_head(head):
        score = lax.dynamic_index_in_dim(scores, head // per_group, 0, keepdims=False)
        level = lax.dynamic_index_in_dim(cumul, head, 1, keepdims=False)
        stride = lax.dynamic_index_in_dim(delta, head, 1, keepdims=False)
        values = lax.dynamic_index_in_dim(x_act, head, 1, keepdims=False)
        spread = jnp.where(live, level[:, None] - level[None, :], 0.0)
        weights = jnp.where(live, score * jnp.exp(spread) * stride[None, :], 0.0).astype(
            jnp.bfloat16
        )
        return jnp.dot(weights, values, preferred_element_type=jnp.float32)

    intra = lax.map(one_head, jnp.arange(head_count, dtype=jnp.int32))
    intra = jnp.transpose(intra, (1, 0, 2))
    last_prompt = prompt_id[row_count - 1]
    final = cumul[row_count - 1]
    keep = (prompt_id == last_prompt)[:, None]
    fade = jnp.where(keep, jnp.exp(jnp.where(keep, final[None, :] - cumul, 0.0)), 0.0)
    inputs = (x_act.astype(jnp.float32) * (delta * fade)[:, :, None]).astype(jnp.bfloat16)
    grouped = inputs.reshape(row_count, group_count, per_group, width)
    ends = jnp.einsum("sgkp,sgn->gkpn", grouped, b_act, preferred_element_type=jnp.float32)
    ends = ends.reshape(head_count, width, state)
    last_start = lax.dynamic_index_in_dim(start_loc, last_prompt, 0, keepdims=False)
    inside = last_start >= 0
    base = lax.dynamic_index_in_dim(
        before_sum, jnp.clip(last_start, 0, row_count - 1), 0, keepdims=False
    )
    carry_in = jnp.exp(jnp.where(inside, final - base, 0.0))
    prefix_last = lax.dynamic_index_in_dim(prefixes, last_prompt, 0, keepdims=False)
    ends = ends + jnp.where(inside, carry_in[:, None, None] * prefix_last, 0.0)
    opens = jnp.any((start_loc >= 0) & (start_loc < row_count))
    through = jnp.where(opens, 0.0, jnp.exp(final))
    return (intra, ends, through, cumul, before_sum)


def span_init(c_act, incoming, prefixes, prompt_id, start_loc, cumul, before_sum):
    row_count, group_count, state = c_act.shape
    prompt_count, head_count, width = (prefixes.shape[0], prefixes.shape[1], prefixes.shape[2])
    per_group = head_count // group_count
    c_wide = c_act.astype(jnp.float32)
    total = jnp.zeros((row_count, head_count, width), jnp.float32)
    for prompt in range(prompt_count):
        begin = start_loc[prompt]
        start_state = jnp.where(begin >= 0, prefixes[prompt], incoming)
        grouped = start_state.reshape(group_count, per_group, width, state)
        reads = jnp.einsum("tgn,gkpn->tgkp", c_wide, grouped, precision=lax.Precision.HIGHEST)
        reads = reads.reshape(row_count, head_count, width)
        base = lax.dynamic_index_in_dim(
            before_sum, jnp.clip(begin, 0, row_count - 1), 0, keepdims=False
        )
        member = (prompt_id == prompt)[:, None]
        fade = jnp.where(member, jnp.exp(jnp.where(member, cumul - base[None, :], 0.0)), 0.0)
        total = total + fade[:, :, None] * reads
    return total


def combine_states(earlier, later):
    return (earlier[0] * later[0], later[0][:, None, None] * earlier[1] + later[1])


def on_device(
    x_mant,
    x_codes,
    bc_raw,
    gate_z,
    conv_x,
    conv_bc,
    dt_raw,
    a_log,
    d_skip,
    norm_gain,
    prompt_lengths,
    cache_slot,
    prefix_state,
    tail_x,
    tail_bc,
):
    row_count = x_mant.shape[0]
    head_count = a_log.shape[0]
    width = x_mant.shape[1] // head_count
    state = prefix_state.shape[2]
    slot_count = prefix_state.shape[0]
    lag_count = tail_x.shape[1]
    prompt_count = prompt_lengths.shape[0]
    heads_group = HEADS // GROUPS
    group_here = max(1, head_count // heads_group)
    per_group = head_count // group_here
    group_cols = GROUPS * state
    ctx_place = lax.axis_index("ctx")
    head_place = lax.axis_index("head")
    offset = ctx_place * row_count
    first_group = head_place * head_count // heads_group
    starts = jnp.cumsum(prompt_lengths) - prompt_lengths
    start_loc = starts - offset
    prompt_id = prompt_rows(starts, offset, row_count)
    x_wide = dequant(x_mant, x_codes)
    x_exact = x_wide.astype(jnp.bfloat16)
    b_first = first_group * state
    c_first = group_cols + first_group * state
    take_cols = group_here * state
    bc_here = jnp.concatenate(
        [
            lax.dynamic_slice_in_dim(bc_raw, b_first, take_cols, 1),
            lax.dynamic_slice_in_dim(bc_raw, c_first, take_cols, 1),
        ],
        axis=1,
    )
    weight_bc = jnp.concatenate(
        [
            lax.dynamic_slice_in_dim(conv_bc, b_first, take_cols, 1),
            lax.dynamic_slice_in_dim(conv_bc, c_first, take_cols, 1),
        ],
        axis=1,
    )
    tail_here = jnp.concatenate(
        [
            lax.dynamic_slice_in_dim(tail_bc, b_first, take_cols, 2),
            lax.dynamic_slice_in_dim(tail_bc, c_first, take_cols, 2),
        ],
        axis=2,
    )
    previous_x, previous_bc = passed_along(
        (x_exact[row_count - lag_count :], bc_here[row_count - lag_count :]), "ctx", 1
    )

    def fetch_one(prompt, buffer_set):
        slot_here = lax.dynamic_index_in_dim(cache_slot, prompt, 0, keepdims=False)
        owner_rank = slot_here // slot_count
        local_index = slot_here % slot_count
        pieces = (
            lax.dynamic_index_in_dim(prefix_state, local_index, 0, keepdims=False),
            lax.dynamic_index_in_dim(tail_x, local_index, 0, keepdims=False),
            lax.dynamic_index_in_dim(tail_here, local_index, 0, keepdims=False),
        )
        arrived = (
            from_root(pieces[0], "ctx", owner_rank),
            from_root(pieces[1], "ctx", owner_rank),
            from_root(pieces[2], "ctx", owner_rank),
        )
        return tuple(
            (
                lax.dynamic_update_index_in_dim(holder, piece, prompt, 0)
                for holder, piece in zip(buffer_set, arrived)
            )
        )

    empty_set = (
        jnp.zeros((prompt_count,) + prefix_state.shape[1:], jnp.bfloat16),
        jnp.zeros((prompt_count,) + tail_x.shape[1:], jnp.bfloat16),
        jnp.zeros((prompt_count,) + tail_here.shape[1:], jnp.bfloat16),
    )
    fetched_state, fetched_x, fetched_bc = lax.fori_loop(0, prompt_count, fetch_one, empty_set)
    prefixes = fetched_state.astype(jnp.float32).reshape(prompt_count, head_count, width, state)
    tails_x = fetched_x.astype(jnp.float32)
    tails_bc = fetched_bc.astype(jnp.float32)
    conv_out = causal_conv(
        x_wide, previous_x.astype(jnp.float32), tails_x, conv_x, prompt_id, start_loc
    )
    x_act = jax.nn.silu(conv_out).astype(jnp.bfloat16).reshape(row_count, head_count, width)
    bc_out = causal_conv(
        bc_here.astype(jnp.float32),
        previous_bc.astype(jnp.float32),
        tails_bc,
        weight_bc,
        prompt_id,
        start_loc,
    )
    bc_act = jax.nn.silu(bc_out).astype(jnp.bfloat16)
    b_act = bc_act[:, :take_cols].reshape(row_count, group_here, state)
    c_act = bc_act[:, take_cols:].reshape(row_count, group_here, state)
    delta = jax.nn.softplus(dt_raw)
    log_decay = -jnp.exp(a_log)[None, :] * delta
    intra, ends, through, cumul, before_sum = span_local(
        x_act, b_act, c_act, delta, log_decay, prompt_id, start_loc, prefixes
    )
    identity = (jnp.ones_like(through), jnp.zeros_like(ends))
    _, incoming = entering((through, ends), "ctx", combine_states, identity)
    init = span_init(c_act, incoming, prefixes, prompt_id, start_loc, cumul, before_sum)
    y_full = intra + init + d_skip[None, :, None] * x_act.astype(jnp.float32)
    gated = y_full * jax.nn.silu(gate_z.astype(jnp.float32).reshape(row_count, head_count, width))
    head_squares = jnp.sum(gated * gated, axis=2)
    local_squares = jnp.sum(head_squares.reshape(row_count, group_here, per_group), axis=2)
    all_groups = lax.dynamic_update_slice_in_dim(
        jnp.zeros((row_count, GROUPS), jnp.float32), local_squares, first_group, 1
    )
    summed = lax.psum(all_groups, "head")
    group_totals = lax.dynamic_slice_in_dim(summed, first_group, group_here, 1)
    inverse = lax.rsqrt(group_totals / (heads_group * width) + eps_norm)
    inverse = jnp.repeat(inverse, per_group, axis=1)
    mixed = gated * inverse[:, :, None] * norm_gain.reshape(head_count, width)[None, :, :]
    return mixed.reshape(row_count, head_count * width).astype(jnp.bfloat16)


def solution(mesh):
    in_specs = (
        P("ctx", "head"),
        P("ctx", "head"),
        P("ctx", None),
        P("ctx", "head"),
        P(None, "head"),
        P(),
        P("ctx", "head"),
        P("head"),
        P("head"),
        P("head"),
        P(),
        P(),
        P("ctx", "head", None),
        P("ctx", None, "head"),
        P("ctx", None, None),
    )
    out_specs = P("ctx", "head")
    return jax.shard_map(
        on_device, mesh=mesh, in_specs=in_specs, out_specs=out_specs, check_vma=False
    )
```

profile of v0, /device:TPU:16, one launch (start us, length us, event | category | flops | bytes accessed | tf_op | source)
XLA Modules:
  0.0 829.4 jit_solution(14115373180927704455)
XLA Ops:
  8.2 1.9 collective-permute-start
  12.9 3.3 collective-permute-start.1
  35.3 558.4 %while.44 = (s32[]{:T(128)}, bf16[4,1024,128]{2,1,0:T(8,128)(2,1)S(1)}, bf16[4,3,1024]{2,1,0:T(4,128)(2,1)S(1)}, bf16[4,3,256]{2,1,0:T(4,128)(2,1)S(1)}, s32[4]{...) while((s32[]{:T(128)}, ...), condition=%wide.region_7.8_spmd, body=%wide.region_3.7_spmd.sunk | while | flops 269851 | bytes 2673102 | solution.py:237
  39.2 1.7 dynamic-slice_select_fusion.6
  40.9 116.9 %all-reduce.2 = (bf16[1,3,1024]{2,1,0:T(4,128)(2,1)S(1)}, bf16[1,3,256]{2,1,0:T(4,128)(2,1)S(1)}) all-reduce(bf16[1,3,1024]{2,1,0:T(4,128)(2,1)S(1)} %dynamic-slice_select_fusion.7, bf16[1,3,256]{2,1,0:T(4,128)(2,1)S(1)} %dynamic-slice_select_fusion.8), channel_id=1, replica_groups=mesh['head'=16,'ctx'=32] {'ctx'}, use_global_device_ids=true, to_apply=%region_5.5 | all-reduce | flops 3840 | bytes 15360 | tf_op jit(solution)/shard_map/while/body/eval_jaxpr/psum | solution.py:19
  157.9 19.0 %all-reduce.5.cloned.1.call-done = bf16[1,1024,128]{2,1,0:T(8,128)(2,1)} async-done(((bf16[1,1024,128]{2,1,0:T(8,128)(2,1)}), bf16[1,1024,128]{2,1,0:T(8,128)(2,1)}) %all-reduce.5.cloned.1.call-update) | async-done | bytes 262160 | tf_op jit(solution)/shard_map/while/body/eval_jaxpr/psum | solution.py:19
  181.7 1.7 dynamic-slice_select_fusion.6
  183.5 117.7 %all-reduce.2 = (bf16[1,3,1024]{2,1,0:T(4,128)(2,1)S(1)}, bf16[1,3,256]{2,1,0:T(4,128)(2,1)S(1)}) all-reduce(bf16[1,3,1024]{2,1,0:T(4,128)(2,1)S(1)} %dynamic-slice_select_fusion.7, bf16[1,3,256]{2,1,0:T(4,128)(2,1)S(1)} %dynamic-slice_select_fusion.8), channel_id=1, replica_groups=mesh['head'=16,'ctx'=32] {'ctx'}, use_global_device_ids=true, to_apply=%region_5.5 | all-reduce | flops 3840 | bytes 15360 | tf_op jit(solution)/shard_map/while/body/eval_jaxpr/psum | solution.py:19
  301.2 14.3 %all-reduce.5.cloned.1.call-done = bf16[1,1024,128]{2,1,0:T(8,128)(2,1)} async-done(((bf16[1,1024,128]{2,1,0:T(8,128)(2,1)}), bf16[1,1024,128]{2,1,0:T(8,128)(2,1)}) %all-reduce.5.cloned.1.call-update) | async-done | bytes 262160 | tf_op jit(solution)/shard_map/while/body/eval_jaxpr/psum | solution.py:19
  320.4 1.7 dynamic-slice_select_fusion.6
  322.1 117.7 %all-reduce.2 = (bf16[1,3,1024]{2,1,0:T(4,128)(2,1)S(1)}, bf16[1,3,256]{2,1,0:T(4,128)(2,1)S(1)}) all-reduce(bf16[1,3,1024]{2,1,0:T(4,128)(2,1)S(1)} %dynamic-slice_select_fusion.7, bf16[1,3,256]{2,1,0:T(4,128)(2,1)S(1)} %dynamic-slice_select_fusion.8), channel_id=1, replica_groups=mesh['head'=16,'ctx'=32] {'ctx'}, use_global_device_ids=true, to_apply=%region_5.5 | all-reduce | flops 3840 | bytes 15360 | tf_op jit(solution)/shard_map/while/body/eval_jaxpr/psum | solution.py:19
  439.8 14.3 %all-reduce.5.cloned.1.call-done = bf16[1,1024,128]{2,1,0:T(8,128)(2,1)} async-done(((bf16[1,1024,128]{2,1,0:T(8,128)(2,1)}), bf16[1,1024,128]{2,1,0:T(8,128)(2,1)}) %all-reduce.5.cloned.1.call-update) | async-done | bytes 262160 | tf_op jit(solution)/shard_map/while/body/eval_jaxpr/psum | solution.py:19
  459.0 1.7 dynamic-slice_select_fusion.6
  460.7 117.7 %all-reduce.2 = (bf16[1,3,1024]{2,1,0:T(4,128)(2,1)S(1)}, bf16[1,3,256]{2,1,0:T(4,128)(2,1)S(1)}) all-reduce(bf16[1,3,1024]{2,1,0:T(4,128)(2,1)S(1)} %dynamic-slice_select_fusion.7, bf16[1,3,256]{2,1,0:T(4,128)(2,1)S(1)} %dynamic-slice_select_fusion.8), channel_id=1, replica_groups=mesh['head'=16,'ctx'=32] {'ctx'}, use_global_device_ids=true, to_apply=%region_5.5 | all-reduce | flops 3840 | bytes 15360 | tf_op jit(solution)/shard_map/while/body/eval_jaxpr/psum | solution.py:19
  578.5 14.3 %all-reduce.5.cloned.1.call-done = bf16[1,1024,128]{2,1,0:T(8,128)(2,1)} async-done(((bf16[1,1024,128]{2,1,0:T(8,128)(2,1)}), bf16[1,1024,128]{2,1,0:T(8,128)(2,1)}) %all-reduce.5.cloned.1.call-update) | async-done | bytes 262160 | tf_op jit(solution)/shard_map/while/body/eval_jaxpr/psum | solution.py:19
  599.9 1.6 gather_fusion.6
  608.0 3.8 multiply_convert_fusion.1
  611.7 1.8 copy.93
  613.5 2.0 fusion.31
  627.5 23.4 %all-gather = f32[32,1,16]{2,1,0:T(1,128)} all-gather(f32[1,1,16]{2,1,0:T(1,128)} %get-tuple-element.529), channel_id=1, replica_groups=mesh['head'=16,'ctx'=32] {'ctx'}, dimensions={0}, use_global_device_ids=true | all-gather | bytes 2112 | tf_op jit(solution)/shard_map/all_gather | solution.py:24
  652.3 73.1 %while.45 = (s32[]{:T(128)}, f32[16,128,64]{1,2,0:T(8,128)}, f32[1,128,128]{2,1,0:T(8,128)S(1)}, s32[16]{0:T(128)S(1)}, f32[128,16]{0,1:T(8,128)}, /*index=5*/f3...) while((s32[]{:T(128)}, f32[16,128,64]{1,2,0:T(8,128)}, ...), condition=%wide.region_10.13_spmd.clone, body=%wide.region_9.12_spmd.clone.sunk | while | flops 2244613 | bytes 119971 | solution.py:98
  725.5 59.8 %while.46 = (s32[]{:T(128)}, f32[16,64,128]{2,1,0:T(8,128)S(1)}, s32[]{:T(128)}, f32[32,16]{1,0:T(8,128)}, f32[32,16,64,128]{3,2,1,0:T(8,128)}, /*index=5*/s32[]{:T(128)}, s32[]{:T(128)}) while((s32[]{:T(128)}, f32[16,64,128]{2,1,0:T(8,128)S(1)}, s32[]{:T(128)}, f32[32,16]{1,0:T(8,128)}, f32[32,16,64,128]{3,2,1,0:T(8,128)}, ...), condition=%wide.region_13.16_spmd.clone, body=%wide.region_12.15_spmd.clone.sunk | while | flops 524292 | bytes 1573161 | solution.py:36
  788.2 1.7 multiply_reduce_fusion
  789.9 31.3 %psum.49 = f32[128,8]{0,1:T(8,128)S(1)} all-reduce(f32[128,8]{0,1:T(8,128)S(1)} %dynamic_update_slice.40), channel_id=1, replica_groups=mesh['head'=16,'ctx'=32] {'head'}, use_global_device_ids=true, to_apply=%region_15.18 | all-reduce | flops 1024 | bytes 8192 | tf_op jit(solution)/shard_map/psum | solution.py:271
  (234 shorter events, 158.8 us)
Async XLA Ops:
  8.2 597.6 %collective-permute-start = (bf16[3,256]{1,0:T(4,128)(2,1)S(1)}, bf16[3,256]{1,0:T(4,128)(2,1)S(1)}, u32[]{:S(2)}, u32[]{:S(2)}) collective-permute-start(bf16[3,256]{1,0:T(4,128)(2,1)S(1)} %fusion.77), channel_id=1, source_target_pairs={{0,1},{1,2},{2,3},{3,4},{4,5},{5,6},{6,7},{7,8},{8,9},{9,10},{10,1... | collective-permute-start | bytes 4616 | tf_op jit(solution)/shard_map/ppermute | solution.py:14
  12.1 0.8 copy-start
  12.9 594.4 %collective-permute-start.1 = (bf16[3,1024]{1,0:T(4,128)(2,1)}, bf16[3,1024]{1,0:T(4,128)(2,1)}, u32[]{:S(2)}, u32[]{:S(2)}) collective-permute-start(bf16[3,1024]{1,0:T(4,128)(2,1)} %slice.281), channel_id=1, source_target_pairs={{0,1},{1,2},{2,3},{3,4},{4,5},{5,6},{6,7},{7,8},{8,9},{9,10},{10,1... | collective-permute-start | bytes 18440 | tf_op jit(solution)/shard_map/ppermute | solution.py:14
  19.1 5.1 copy-start.3
  35.3 141.5 %all-reduce.5.cloned.1.call-start = ((), (), s32[]{:S(2)}) async-start(), calls=%async_computation.1 | async-start | bytes 524288 | tf_op jit(solution)/shard_map/while/body/eval_jaxpr/psum | solution.py:19
  177.8 137.6 %all-reduce.5.cloned.1.call-start = ((), (), s32[]{:S(2)}) async-start(), calls=%async_computation.1 | async-start | bytes 524288 | tf_op jit(solution)/shard_map/while/body/eval_jaxpr/psum | solution.py:19
  316.5 137.6 %all-reduce.5.cloned.1.call-start = ((), (), s32[]{:S(2)}) async-start(), calls=%async_computation.1 | async-start | bytes 524288 | tf_op jit(solution)/shard_map/while/body/eval_jaxpr/psum | solution.py:19
  455.1 137.6 %all-reduce.5.cloned.1.call-start = ((), (), s32[]{:S(2)}) async-start(), calls=%async_computation.1 | async-start | bytes 524288 | tf_op jit(solution)/shard_map/while/body/eval_jaxpr/psum | solution.py:19
  593.7 131.7 %all-gather.3.cloned.1.call-start = ((), (), s32[]{:S(2)}) async-start(), calls=%async_computation | async-start | bytes 17301504 | tf_op jit(solution)/shard_map/all_gather | solution.py:24
  652.3 168.9 %copy-start.2 = (f32[16,64]{1,0:T(8,128)S(1)}, f32[16,64]{1,0:T(8,128)}, u32[]{:S(2)}) copy-start(f32[16,64]{1,0:T(8,128)} %mul.333) | copy-start | bytes 12292
  725.4 62.7 %copy-start.1 = (bf16[128,16,64]{0,2,1:T(8,128)(2,1)}, bf16[128,16,64]{0,2,1:T(8,128)(2,1)S(1)}, u32[]{:S(2)}) copy-start(bf16[128,16,64]{0,2,1:T(8,128)(2,1)S(1)} %get-tuple-element.805) | copy-start | bytes 786436
Sparse Core Ops, SparseCore 0:
  41.0 135.7 all-reduce.4
  183.6 131.8 all-reduce.4
  322.2 131.8 all-reduce.4
  460.8 131.8 all-reduce.4
Sparse Core Ops, SparseCore 1:
  615.6 87.8 all-gather.2
where the time goes:
time: 835 us; the launch traced here: 829 us
  blocking collectives  525 us (63%)
  local copies, waits for them, and re-layouts  83.4 us (10%)
  waiting for transfers between devices  61.8 us (7%)
  other arithmetic  60.6 us (7%)
  loops' own time  38.6 us (5%)
  matrix products  32 us (4%)
  between operations  23 us (3%)
    psum x4, blocking collectives, from_root(): return lax.psum(kept, axis)  470 us
    psum x4, waiting for transfers between devices, from_root(): return lax.psum(kept, axis)  61.7 us
    select_n x32, other arithmetic, hop(): return jax.tree.map(lambda a, b: jnp.where(reached, a, b), new, before)  37.4 us
    psum x1, blocking collectives, on_device(): summed = lax.psum(all_groups, 'head')  31.3 us
    another operation x1, loops' own time, span_local(): intra = lax.map(one_head, jnp.arange(head_count, dtype=jnp.int32))  27.3 us
    dot_general x16, matrix products, one_head(): return jnp.dot(weights, values, preferred_element_type=jnp.float32)  25.3 us
    all_gather x1, blocking collectives, entering(): everything = jax.tree.map(lambda part: lax.all_gather(part, axis), array)  23.4 us
    mul x32, local copies, waits for them, and re-layouts, combine_states(): later[0][:, None, None] * earlier[1] + later[1]  21.8 us
  transfers between devices with their start and end apart: 7, of which 4 were waited for; matrix products, arithmetic and copies ran while one was open for 12% of the time, Pallas kernels for 0%

commit v1 on v0

--- a/solution.py
+++ b/solution.py
@@ -16,7 +16,7 @@
 
 def from_root(value, axis, source):
     kept = jnp.where(lax.axis_index(axis) == source, value, 0).astype(value.dtype)
-    return lax.psum(kept, axis)
+    return jnp.sum(lax.all_gather(kept, axis_name=axis), axis=0)
 
 
 def entering(array, axis, combine, identity):

time: 835 us -> 593 us (0.71)
  the two profiles are of different devices: /device:TPU:16 before, /device:TPU:2 now
where the time goes in v1:
time: 593 us; the launch traced here: 588 us
  blocking collectives  239 us (40%)
  waiting for transfers between devices  91.5 us (15%)
  other arithmetic  80.6 us (14%)
  local copies, waits for them, and re-layouts  79.9 us (13%)
  loops' own time  38.2 us (6%)
  matrix products  30.5 us (5%)
  between operations  23.2 us (4%)
    all_gather x8, blocking collectives, from_root(): return jnp.sum(lax.all_gather(kept, axis_name=axis), axis=0)  185 us
    all_gather x4, waiting for transfers between devices, from_root(): return jnp.sum(lax.all_gather(kept, axis_name=axis), axis=0)  91.4 us
    select_n x32, other arithmetic, hop(): return jax.tree.map(lambda a, b: jnp.where(reached, a, b), new, before)  37.4 us
    psum x1, blocking collectives, on_device(): summed = lax.psum(all_groups, 'head')  31.3 us
    another operation x1, loops' own time, span_local(): intra = lax.map(one_head, jnp.arange(head_count, dtype=jnp.int32))  26.9 us
    dot_general x16, matrix products, one_head(): return jnp.dot(weights, values, preferred_element_type=jnp.float32)  24.9 us
    all_gather x1, blocking collectives, entering(): everything = jax.tree.map(lambda part: lax.all_gather(part, axis), array)  22.3 us
    mul x32, local copies, waits for them, and re-layouts, combine_states(): later[0][:, None, None] * earlier[1] + later[1]  22 us
  transfers between devices with their start and end apart: 7, of which 4 were waited for; matrix products, arithmetic and copies ran while one was open for 20% of the time, Pallas kernels for 0%

profile of v1, /device:TPU:2, one launch (start us, length us, event | category | flops | bytes accessed | tf_op | source)
XLA Modules:
  0.0 588.1 jit_solution(11985059383814895099)
XLA Ops:
  12.9 3.6 collective-permute-start.1
  36.0 319.0 %while.45 = (s32[]{:T(128)}, bf16[4,1024,128]{2,1,0:T(8,128)(2,1)S(1)}, bf16[4,3,1024]{2,1,0:T(4,128)(2,1)S(1)}, bf16[4,3,256]{2,1,0:T(4,128)(2,1)S(1)}, s32[4]{...) while((s32[]{:T(128)}, ...), condition=%wide.region_7.8_spmd, body=%wide.region_3.7_spmd.sunk | while | flops 4317211 | bytes 36194772 | solution.py:237
  41.6 25.3 %all_gather.56 = bf16[32,3,1024]{2,1,0:T(4,128)(2,1)S(1)} all-gather(bf16[1,3,1024]{2,1,0:T(4,128)(2,1)S(1)} %dynamic-slice_select_fusion.7), channel_id=1, replica_groups=mesh['head'=16,'ctx'=32] {'ctx'}, dimensions={0}, use_global_device_ids=true | all-gather | bytes 202752 | tf_op jit(solution)/shard_map/while/body/eval_jaxpr/all_gather | solution.py:19
  67.0 21.5 %all_gather.57 = bf16[32,3,256]{2,1,0:T(4,128)(2,1)S(1)} all-gather(bf16[1,3,256]{2,1,0:T(4,128)(2,1)S(1)} %dynamic-slice_select_fusion.8), channel_id=1, replica_groups=mesh['head'=16,'ctx'=32] {'ctx'}, dimensions={0}, use_global_device_ids=true | all-gather | bytes 50688 | tf_op jit(solution)/shard_map/while/body/eval_jaxpr/all_gather | solution.py:19
  88.6 25.7 %all-gather.6.cloned.1.call-done = bf16[32,1024,128]{2,1,0:T(8,128)(2,1)} async-done(((bf16[1,1024,128]{2,1,0:T(8,128)(2,1)}), bf16[32,1024,128]{2,1,0:T(8,128)(2,1)}) %all-gather.6.cloned.1.call-update) | async-done | bytes 8388624 | tf_op jit(solution)/shard_map/while/body/eval_jaxpr/all_gather | solution.py:19
  114.3 4.7 reduce_sum.89
  124.7 23.2 %all_gather.56 = bf16[32,3,1024]{2,1,0:T(4,128)(2,1)S(1)} all-gather(bf16[1,3,1024]{2,1,0:T(4,128)(2,1)S(1)} %dynamic-slice_select_fusion.7), channel_id=1, replica_groups=mesh['head'=16,'ctx'=32] {'ctx'}, dimensions={0}, use_global_device_ids=true | all-gather | bytes 202752 | tf_op jit(solution)/shard_map/while/body/eval_jaxpr/all_gather | solution.py:19
  148.0 22.9 %all_gather.57 = bf16[32,3,256]{2,1,0:T(4,128)(2,1)S(1)} all-gather(bf16[1,3,256]{2,1,0:T(4,128)(2,1)S(1)} %dynamic-slice_select_fusion.8), channel_id=1, replica_groups=mesh['head'=16,'ctx'=32] {'ctx'}, dimensions={0}, use_global_device_ids=true | all-gather | bytes 50688 | tf_op jit(solution)/shard_map/while/body/eval_jaxpr/all_gather | solution.py:19
  171.0 21.9 %all-gather.6.cloned.1.call-done = bf16[32,1024,128]{2,1,0:T(8,128)(2,1)} async-done(((bf16[1,1024,128]{2,1,0:T(8,128)(2,1)}), bf16[32,1024,128]{2,1,0:T(8,128)(2,1)}) %all-gather.6.cloned.1.call-update) | async-done | bytes 8388624 | tf_op jit(solution)/shard_map/while/body/eval_jaxpr/all_gather | solution.py:19
  192.9 4.7 reduce_sum.89
  203.4 23.2 %all_gather.56 = bf16[32,3,1024]{2,1,0:T(4,128)(2,1)S(1)} all-gather(bf16[1,3,1024]{2,1,0:T(4,128)(2,1)S(1)} %dynamic-slice_select_fusion.7), channel_id=1, replica_groups=mesh['head'=16,'ctx'=32] {'ctx'}, dimensions={0}, use_global_device_ids=true | all-gather | bytes 202752 | tf_op jit(solution)/shard_map/while/body/eval_jaxpr/all_gather | solution.py:19
  226.7 22.9 %all_gather.57 = bf16[32,3,256]{2,1,0:T(4,128)(2,1)S(1)} all-gather(bf16[1,3,256]{2,1,0:T(4,128)(2,1)S(1)} %dynamic-slice_select_fusion.8), channel_id=1, replica_groups=mesh['head'=16,'ctx'=32] {'ctx'}, dimensions={0}, use_global_device_ids=true | all-gather | bytes 50688 | tf_op jit(solution)/shard_map/while/body/eval_jaxpr/all_gather | solution.py:19
  249.7 21.9 %all-gather.6.cloned.1.call-done = bf16[32,1024,128]{2,1,0:T(8,128)(2,1)} async-done(((bf16[1,1024,128]{2,1,0:T(8,128)(2,1)}), bf16[32,1024,128]{2,1,0:T(8,128)(2,1)}) %all-gather.6.cloned.1.call-update) | async-done | bytes 8388624 | tf_op jit(solution)/shard_map/while/body/eval_jaxpr/all_gather | solution.py:19
  271.6 4.7 reduce_sum.89
  282.0 23.2 %all_gather.56 = bf16[32,3,1024]{2,1,0:T(4,128)(2,1)S(1)} all-gather(bf16[1,3,1024]{2,1,0:T(4,128)(2,1)S(1)} %dynamic-slice_select_fusion.7), channel_id=1, replica_groups=mesh['head'=16,'ctx'=32] {'ctx'}, dimensions={0}, use_global_device_ids=true | all-gather | bytes 202752 | tf_op jit(solution)/shard_map/while/body/eval_jaxpr/all_gather | solution.py:19
  305.4 22.9 %all_gather.57 = bf16[32,3,256]{2,1,0:T(4,128)(2,1)S(1)} all-gather(bf16[1,3,256]{2,1,0:T(4,128)(2,1)S(1)} %dynamic-slice_select_fusion.8), channel_id=1, replica_groups=mesh['head'=16,'ctx'=32] {'ctx'}, dimensions={0}, use_global_device_ids=true | all-gather | bytes 50688 | tf_op jit(solution)/shard_map/while/body/eval_jaxpr/all_gather | solution.py:19
  328.3 21.9 %all-gather.6.cloned.1.call-done = bf16[32,1024,128]{2,1,0:T(8,128)(2,1)} async-done(((bf16[1,1024,128]{2,1,0:T(8,128)(2,1)}), bf16[32,1024,128]{2,1,0:T(8,128)(2,1)}) %all-gather.6.cloned.1.call-update) | async-done | bytes 8388624 | tf_op jit(solution)/shard_map/while/body/eval_jaxpr/all_gather | solution.py:19
  350.2 4.7 reduce_sum.89
  369.3 4.0 multiply_convert_fusion.1
  375.0 2.0 fusion.31
  389.0 22.3 %all-gather = f32[32,1,16]{2,1,0:T(1,128)} all-gather(f32[1,1,16]{2,1,0:T(1,128)} %get-tuple-element.543), channel_id=1, replica_groups=mesh['head'=16,'ctx'=32] {'ctx'}, dimensions={0}, use_global_device_ids=true | all-gather | bytes 2112 | tf_op jit(solution)/shard_map/all_gather | solution.py:24
  412.7 72.3 %while.46 = (s32[]{:T(128)}, f32[16,128,64]{1,2,0:T(8,128)}, f32[1,128,128]{2,1,0:T(8,128)S(1)}, s32[16]{0:T(128)S(1)}, f32[128,16]{0,1:T(8,128)}, /*index=5*/f3...) while((s32[]{:T(128)}, f32[16,128,64]{1,2,0:T(8,128)}, ...), condition=%wide.region_10.13_spmd.clone, body=%wide.region_9.12_spmd.clone.sunk | while | flops 2244613 | bytes 119971 | solution.py:98
  485.0 60.0 %while.47 = (s32[]{:T(128)}, f32[16,64,128]{2,1,0:T(8,128)S(1)}, s32[]{:T(128)}, f32[32,16]{1,0:T(8,128)}, f32[32,16,64,128]{3,2,1,0:T(8,128)}, /*index=5*/s32[]{:T(128)}, s32[]{:T(128)}) while((s32[]{:T(128)}, f32[16,64,128]{2,1,0:T(8,128)S(1)}, s32[]{:T(128)}, f32[32,16]{1,0:T(8,128)}, f32[32,16,64,128]{3,2,1,0:T(8,128)}, ...), condition=%wide.region_13.16_spmd.clone, body=%wide.region_12.15_spmd.clone.sunk | while | flops 524292 | bytes 1573161 | solution.py:36
  548.6 31.3 %psum.7 = f32[128,8]{0,1:T(8,128)S(1)} all-reduce(f32[128,8]{0,1:T(8,128)S(1)} %dynamic_update_slice.43), channel_id=1, replica_groups=mesh['head'=16,'ctx'=32] {'head'}, use_global_device_ids=true, to_apply=%region_15.18 | all-reduce | flops 1024 | bytes 8192 | tf_op jit(solution)/shard_map/psum | solution.py:271
  (254 shorter events, 168.3 us)
Async XLA Ops:
  8.2 358.9 %collective-permute-start = (bf16[3,256]{1,0:T(4,128)(2,1)S(1)}, bf16[3,256]{1,0:T(4,128)(2,1)S(1)}, u32[]{:S(2)}, u32[]{:S(2)}) collective-permute-start(bf16[3,256]{1,0:T(4,128)(2,1)S(1)} %fusion.77), channel_id=1, source_target_pairs={{0,1},{1,2},{2,3},{3,4},{4,5},{5,6},{6,7},{7,8},{8,9},{9,10},{10,1... | collective-permute-start | bytes 4616 | tf_op jit(solution)/shard_map/ppermute | solution.py:14
  12.1 0.8 copy-start
  12.9 355.6 %collective-permute-start.1 = (bf16[3,1024]{1,0:T(4,128)(2,1)}, bf16[3,1024]{1,0:T(4,128)(2,1)}, u32[]{:S(2)}, u32[]{:S(2)}) collective-permute-start(bf16[3,1024]{1,0:T(4,128)(2,1)} %slice.281), channel_id=1, source_target_pairs={{0,1},{1,2},{2,3},{3,4},{4,5},{5,6},{6,7},{7,8},{8,9},{9,10},{10,1... | collective-permute-start | bytes 18440 | tf_op jit(solution)/shard_map/ppermute | solution.py:14
  19.4 5.4 copy-start.5
  36.0 78.2 %all-gather.6.cloned.1.call-start = ((), (), s32[]{:S(2)}) async-start(), calls=%async_computation.1 | async-start | bytes 8650752 | tf_op jit(solution)/shard_map/while/body/eval_jaxpr/all_gather | solution.py:19
  119.1 73.8 %all-gather.6.cloned.1.call-start = ((), (), s32[]{:S(2)}) async-start(), calls=%async_computation.1 | async-start | bytes 8650752 | tf_op jit(solution)/shard_map/while/body/eval_jaxpr/all_gather | solution.py:19
  197.7 73.8 %all-gather.6.cloned.1.call-start = ((), (), s32[]{:S(2)}) async-start(), calls=%async_computation.1 | async-start | bytes 8650752 | tf_op jit(solution)/shard_map/while/body/eval_jaxpr/all_gather | solution.py:19
  276.4 73.8 %all-gather.6.cloned.1.call-start = ((), (), s32[]{:S(2)}) async-start(), calls=%async_computation.1 | async-start | bytes 8650752 | tf_op jit(solution)/shard_map/while/body/eval_jaxpr/all_gather | solution.py:19
  355.1 129.9 %all-gather.4.cloned.1.call-start = ((), (), s32[]{:S(2)}) async-start(), calls=%async_computation | async-start | bytes 17301504 | tf_op jit(solution)/shard_map/all_gather | solution.py:24
  412.3 132.6 %copy-start.1 = (f32[1,1024,128]{2,1,0:T(8,128)S(1)}, f32[1,1024,128]{2,1,0:T(8,128)}, u32[]{:S(2)}) copy-start(f32[1,1024,128]{2,1,0:T(8,128)} %get-tuple-element.527) | copy-start | bytes 1572868
  412.7 132.3 %copy-start.3 = (f32[128,16]{0,1:T(8,128)S(1)}, f32[128,16]{0,1:T(8,128)}, u32[]{:S(2)}) copy-start(f32[128,16]{0,1:T(8,128)} %copy.92) | copy-start | bytes 24580
  485.0 60.0 %copy-start.2 = (bf16[128,16,64]{0,2,1:T(8,128)(2,1)}, bf16[128,16,64]{0,2,1:T(8,128)(2,1)S(1)}, u32[]{:S(2)}) copy-start(bf16[128,16,64]{0,2,1:T(8,128)(2,1)S(1)} %get-tuple-element.818) | copy-start | bytes 786436
  485.0 95.0 %copy-start.4 = (f32[16,64]{1,0:T(8,128)S(1)}, f32[16,64]{1,0:T(8,128)}, u32[]{:S(2)}) copy-start(f32[16,64]{1,0:T(8,128)} %mul.333) | copy-start | bytes 12292
Sparse Core Ops, SparseCore 0:
  41.7 72.5 all-gather.5
  124.8 68.0 all-gather.5
  203.5 68.0 all-gather.5
  282.1 68.0 all-gather.5
Sparse Core Ops, SparseCore 1:
  377.1 87.5 all-gather.3
